TPU v7x, 512 devices: a whole 4x4x16 slice. The times are simulated.
512 devices in a mesh: grid: 32 (over x, y, core), band: 16 (over z).
Axes of the slice: x: 4, y: 4, z: 16, core: 2. Of those that a mesh axis runs over, the one named last changes fastest.
Arguments:
- orbitals: bfloat16 [32768, 512], P('grid', 'band'), may hold values from -6 to 6
- rotation: bfloat16 [512, 32768], P('grid', 'band'), may hold values from -0.25 to 0.25
Outputs:
- rotated: bfloat16 [32768, 32768], P('grid', 'band')
All inputs are finite; a program needn't handle non-finite values.
Results may differ from a plain program's by a relative error of at most 0.001.
Values may be sent and summed in bfloat16 or wider, within the bound.
No kernel may reach another device: no remote copies, remote signals or barrier semaphores. Data moves between devices by JAX's collectives and lax.ppermute only.
A program may use at most 64 MiB of HBM per device.

v0:
```python
import jax
import jax.numpy as jnp
from jax import lax
from jax.sharding import PartitionSpec as P


def on_device(orbitals, rotation):
    all_cols = lax.all_gather(orbitals, "band", axis=1, tiled=True)
    all_rows = lax.all_gather(rotation, "grid", axis=0, tiled=True)
    total = jnp.dot(all_cols, all_rows, preferred_element_type=jnp.float32)
    return total.astype(jnp.bfloat16)


def solution(mesh):
    in_specs = (P("grid", "band"), P("grid", "band"))
    out_specs = P("grid", "band")
    return jax.shard_map(
        on_device, mesh=mesh, in_specs=in_specs, out_specs=out_specs, check_vma=False
    )
```

profile of v0, /device:TPU:6, one launch (start us, length us, event | category | flops | bytes accessed | tf_op | source)
XLA Modules:
  0.0 156.8 jit_solution(7569212816232975436)
XLA Ops:
  6.5 0.0 all-gather.3.cloned.1.call-start
  6.5 0.7 all-gather.3.cloned.1.call-update
  7.3 0.0 all-gather.5.cloned.1.call-start
  7.3 0.7 all-gather.5.cloned.1.call-update
  8.0 76.9 %all-gather.3.cloned.1.call-done = bf16[1024,512]{0,1:T(8,128)(2,1)} async-done(((bf16[1024,32]{0,1:T(8,128)(2,1)}), bf16[1024,512]{0,1:T(8,128)(2,1)}) %all-gather.3.cloned.1.call-update) | async-done | bytes 1048592 | tf_op jit(solution)/shard_map/all_gather | solution.py:8
  84.9 58.8 %all-gather.5.cloned.1.call-done = bf16[512,2048]{1,0:T(8,128)(2,1)} async-done(((bf16[16,2048]{1,0:T(8,128)(2,1)}), bf16[512,2048]{1,0:T(8,128)(2,1)}) %all-gather.5.cloned.1.call-update) | async-done | bytes 2097168 | tf_op jit(solution)/shard_map/all_gather | solution.py:9
  143.7 6.3 %convolution_convert_fusion = bf16[1024,2048]{1,0:T(8,128)(2,1)} fusion(bf16[1024,512]{0,1:T(8,128)(2,1)} %all-gather.3.cloned.1.call-done, bf16[512,2048]{1,0:T(8,128)(2,1)} %all-gather.5.cloned.1.call-done), kind=kOutput, calls=%fused_computation | convolution fusion | flops 2149580800 | bytes 7340032 | tf_op jit(solution)/shard_map/dot_general | solution.py:10
Async XLA Ops:
  6.5 78.4 %all-gather.3.cloned.1.call-start = ((), (), s32[]{:S(2)}) async-start(), calls=%async_computation | async-start | bytes 1114112 | tf_op jit(solution)/shard_map/all_gather | solution.py:8
  7.3 136.4 %all-gather.5.cloned.1.call-start = ((), (), s32[]{:S(2)}) async-start(), calls=%async_computation.1 | async-start | bytes 2162688 | tf_op jit(solution)/shard_map/all_gather | solution.py:9
Sparse Core Ops, SparseCore 0:
  9.4 75.4 all-gather.2
  88.0 55.5 all-gather.4
where the time goes:
time: 159 us; the launch traced here: 157 us
  waiting for transfers between devices  137 us (86%)
  between operations  13.4 us (8%)
  matrix products  6.32 us (4%)
    all_gather x1, waiting for transfers between devices, on_device(): all_cols = lax.all_gather(orbitals, 'band', axis=1, tiled=True)  76.9 us
    all_gather x1, waiting for transfers between devices, on_device(): all_rows = lax.all_gather(rotation, 'grid', axis=0, tiled=True)  58.8 us
    dot_general x1, matrix products, on_device(): total = jnp.dot(all_cols, all_rows, preferred_element_type=jnp.float32)  6.32 us
  transfers between devices with their start and end apart: 2, of which 2 were waited for; matrix products, arithmetic and copies ran while one was open for 0% of the time, Pallas kernels for 0%

commit v1 on v0

v1 whole, which is shorter than its diff:
```python
import jax
import jax.numpy as jnp
from jax import lax
from jax.sharding import PartitionSpec as P

ALONE = 896


def spread(block, axis):
    n = lax.axis_size(axis)
    copies = jnp.broadcast_to(block[None], (n, *block.shape))
    return lax.all_to_all(copies, axis, 0, 0, tiled=True).reshape(-1, block.shape[1])


def on_device(orbitals, rotation):
    columns = orbitals.T
    all_rows = spread(rotation, "grid")
    rest = spread(columns[:, ALONE:], "band")
    main = lax.all_gather(columns[:, :ALONE], "band", axis=0, tiled=True)
    all_cols = jnp.concatenate([main, rest], axis=1)
    total = lax.dot_general(
        all_cols, all_rows, (((0,), (0,)), ((), ())), preferred_element_type=jnp.float32
    )
    return total.astype(jnp.bfloat16)


def solution(mesh):
    in_specs = (P("grid", "band"), P("grid", "band"))
    out_specs = P("grid", "band")
    return jax.shard_map(
        on_device, mesh=mesh, in_specs=in_specs, out_specs=out_specs, check_vma=False
    )
```

time: 159 us -> 79.2 us (0.50); the launches traced: 157 us -> 78.8 us
  waiting for transfers between devices: 137 us -> 0.01 us
  blocking collectives: 0 us -> 63.5 us
  between operations: 13.4 us -> 0.03 us
  starting transfers between devices: 0.04 us -> 7.74 us
  local copies, waits for them, and re-layouts: 0 us -> 3.14 us
  matrix products: 6.32 us -> 4.39 us
    all_gather x2 -> x0, waiting for transfers between devices: 136 us -> none  [the longest x1 76.9 us: on_device(): all_cols = lax.all_gather(orbitals, 'band', axis=1, tiled=True)]
    all_gather x0 -> x1, blocking collectives: none -> 33.8 us  [on_device(): main = lax.all_gather(columns[:, :ALONE], 'band', axis=0, tiled=True)]
    all_to_all x0 -> x1, blocking collectives: none -> 29.7 us  [spread(): lax.all_to_all(copies, axis, 0, 0, tiled=True).reshape(-1, block.shape[1])]
    all_to_all x0 -> x1, starting transfers between devices: none -> 7.74 us  [spread(): lax.all_to_all(copies, axis, 0, 0, tiled=True).reshape(-1, block.shape[1])]
    broadcast_in_dim x0 -> x2, local copies, waits for them, and re-layouts: none -> 2.43 us  [spread(): copies = jnp.broadcast_to(block[None], (n, *block.shape))]
    dot_general x1, matrix products: 6.32 us -> 4.39 us  [on_device(): lax.dot_general(all_cols, all_rows, (((0,), (0,)), ((), ())), preferred_e...]
  transfers between devices with their start and end apart: 2 -> 1, of which waited for: 2 -> 0; matrix products, arithmetic and copies ran while one was open for 0% -> 0% of each run, Pallas kernels for 0% -> 0%
where the time goes in v1:
time: 79.2 us; the launch traced here: 78.8 us
  blocking collectives  63.5 us (80%)
  starting transfers between devices  7.74 us (10%)
  matrix products  4.39 us (6%)
  local copies, waits for them, and re-layouts  3.14 us (4%)
    all_gather x1, blocking collectives, on_device(): main = lax.all_gather(columns[:, :ALONE], 'band', axis=0, tiled=True)  33.8 us
    all_to_all x1, blocking collectives, spread(): lax.all_to_all(copies, axis, 0, 0, tiled=True).reshape(-1, block.shape[1])  29.7 us
    all_to_all x1, starting transfers between devices, spread(): lax.all_to_all(copies, axis, 0, 0, tiled=True).reshape(-1, block.shape[1])  7.74 us
    dot_general x1, matrix products, on_device(): lax.dot_general(all_cols, all_rows, (((0,), (0,)), ((), ())), preferred_e...  4.39 us
    broadcast_in_dim x2, local copies, waits for them, and re-layouts, spread(): copies = jnp.broadcast_to(block[None], (n, *block.shape))  2.43 us
  transfers between devices with their start and end apart: 1, of which 0 were waited for; matrix products, arithmetic and copies ran while one was open for 0% of the time, Pallas kernels for 0%

profile of v1, /device:TPU:6, one launch (start us, length us, event | category | flops | bytes accessed | tf_op | source)
XLA Modules:
  0.0 78.8 jit_solution(8730877428883429115)
XLA Ops:
  0.0 0.7 slice.9
  0.7 29.7 %all_to_all.10 = bf16[16,32,128]{2,1,0:T(8,128)(2,1)S(1)} all-to-all(bf16[16,32,128]{2,1,0:T(8,128)(2,1)S(1)} %broadcast_in_dim.4), channel_id=1, replica_groups=mesh['grid'=32,'band'=16] {'band'}, dimensions={0} | all-to-all | bytes 262144 | tf_op jit(solution)/shard_map/all_to_all | solution.py:12
  30.4 2.4 %broadcast_in_dim.5 = bf16[32,16,2048]{2,1,0:T(8,128)(2,1)} broadcast(bf16[16,2048]{1,0:T(8,128)(2,1)} %param.3), dimensions={1,2} | broadcast | bytes 2162688 | tf_op jit(solution)/shard_map/broadcast_in_dim | solution.py:11
  32.8 0.0 copy-start
  32.8 7.7 %all-to-all-start.1 = ((bf16[32,16,2048]{2,1,0:T(8,128)(2,1)}), bf16[32,16,2048]{2,1,0:T(8,128)(2,1)S(1)}, u32[]{:S(2)}, u32[]{:S(2)}) async-start(bf16[32,16,2048]{2,1,0:T(8,128)(2,1)} %broadcast_in_dim.5), calls=%async_computation.1 | async-start | bytes 4194304 | tf_op jit(solution)/shard_map/all_to_all | solution.py:12
  40.6 0.0 copy-done
  40.6 33.8 %all_gather.3 = bf16[512,896]{1,0:T(8,128)(2,1)S(1)} all-gather(bf16[32,896]{1,0:T(8,128)(2,1)S(1)} %slice.8), channel_id=1, replica_groups=mesh['grid'=32,'band'=16] {'band'}, dimensions={0}, use_global_device_ids=true | all-gather | bytes 974848 | tf_op jit(solution)/shard_map/all_gather | solution.py:19
  74.4 0.0 all-to-all-done.1
  74.4 4.4 %convolution_convert_fusion = bf16[1024,2048]{1,0:T(8,128)(2,1)} fusion(bf16[512,2048]{1,0:T(8,128)(2,1)S(1)} %bitcast.4, bf16[512,128]{1,0:T(8,128)(2,1)S(1)} %bitcast.5, bf16[512,896]{1,0:T(8,128)(2,1)S(1)} %all_gather.3), kind=kOutput, calls=%fused_computation | convolution fusion | flops 2151677952 | bytes 7340032 | tf_op jit(solution)/shard_map/dot_general | solution.py:21
  (2 shorter events, 0.0 us)
Async XLA Ops:
  32.8 7.8 %copy-start = (bf16[1024,32]{0,1:T(8,128)(2,1)S(1)}, bf16[1024,32]{0,1:T(8,128)(2,1)}, u32[]{:S(2)}) copy-start(bf16[1024,32]{0,1:T(8,128)(2,1)} %param.2) | copy-start | bytes 196612
  32.8 41.6 %all-to-all-start.1 = ((bf16[32,16,2048]{2,1,0:T(8,128)(2,1)}), bf16[32,16,2048]{2,1,0:T(8,128)(2,1)S(1)}, u32[]{:S(2)}, u32[]{:S(2)}) async-start(bf16[32,16,2048]{2,1,0:T(8,128)(2,1)} %broadcast_in_dim.5), calls=%async_computation.1 | async-start | bytes 4194304 | tf_op jit(solution)/shard_map/all_to_all | solution.py:12

commit v2 on v0

v2 whole, which is shorter than its diff:
```python
import jax
import jax.numpy as jnp
from jax import lax
from jax.experimental import pallas as pl
from jax.experimental.pallas import tpu as pltpu
from jax.sharding import Mesh
from jax.sharding import PartitionSpec as P

GRID = ("x", "y", "core")
PAIRS, PARITY = "pairs", "parity"
BAND = (PAIRS, PARITY)
VMEM = pl.BlockSpec(memory_space=pltpu.VMEM)
TILE = 512


def params(mib):
    return pltpu.CompilerParams(vmem_limit_bytes=mib << 20)


def copies_of(block, n):
    def kernel(block_ref, out_ref):
        held = block_ref[...]
        for i in range(n):
            out_ref[i] = held

    return pl.pallas_call(
        kernel,
        out_shape=jax.ShapeDtypeStruct((n, *block.shape), block.dtype),
        in_specs=[VMEM],
        out_specs=VMEM,
        compiler_params=params(8),
    )(block)


def turned(cols):
    k, points = cols.shape
    half = points // 2

    def kernel(cols_ref, upper_ref, lower_ref):
        for i in range(0, half, 128):
            upper_ref[i : i + 128, :] = cols_ref[:, i : i + 128].T
            lower_ref[i : i + 128, :] = cols_ref[:, half + i : half + i + 128].T

    shape = jax.ShapeDtypeStruct((half, k), cols.dtype)
    return pl.pallas_call(
        kernel,
        out_shape=(shape, shape),
        in_specs=[VMEM],
        out_specs=(VMEM, VMEM),
        compiler_params=params(8),
    )(cols)


def first_sum(upper, lower, rows):
    half, k = upper.shape
    n = rows.shape[1]

    def kernel(upper_ref, lower_ref, rows_ref, sum_ref):
        for h, part in enumerate((upper_ref, lower_ref)):
            for c in range(0, n, TILE):
                sum_ref[h * half : (h + 1) * half, c : c + TILE] = jnp.dot(
                    part[...],
                    rows_ref[:, c : c + TILE],
                    preferred_element_type=jnp.float32,
                )

    return pl.pallas_call(
        kernel,
        out_shape=jax.ShapeDtypeStruct((2 * half, n), jnp.float32),
        in_specs=[VMEM] * 3,
        out_specs=VMEM,
        compiler_params=params(12),
        cost_estimate=pl.CostEstimate(
            flops=4 * half * k * n, bytes_accessed=8 * half * n, transcendentals=0
        ),
    )(upper, lower, rows)


def finished(total, upper, lower, rows):
    half, k = upper.shape
    n = rows.shape[1]
    tiles = [(h, c) for h in range(2) for c in range(0, n, TILE)]

    def kernel(total_ref, upper_ref, lower_ref, rows_ref, out_ref, held, sems):
        copies = []
        for t, (h, c) in enumerate(tiles):
            part = (upper_ref, lower_ref)[h]
            where = (slice(h * half, (h + 1) * half), slice(c, c + TILE))
            held[t] = (
                total_ref[where]
                + jnp.dot(
                    part[...],
                    rows_ref[:, c : c + TILE],
                    preferred_element_type=jnp.float32,
                )
            ).astype(jnp.bfloat16)
            copies.append(
                pltpu.make_async_copy(held.at[t], out_ref.at[where], sems.at[t])
            )
            copies[-1].start()
        for copy in copies:
            copy.wait()

    return pl.pallas_call(
        kernel,
        out_shape=jax.ShapeDtypeStruct((2 * half, n), jnp.bfloat16),
        in_specs=[VMEM] * 4,
        out_specs=pl.BlockSpec(memory_space=pl.ANY),
        scratch_shapes=[
            pltpu.VMEM((len(tiles), half, TILE), jnp.bfloat16),
            pltpu.SemaphoreType.DMA((len(tiles),)),
        ],
        compiler_params=params(24),
        cost_estimate=pl.CostEstimate(
            flops=4 * half * k * n, bytes_accessed=12 * half * n, transcendentals=0
        ),
    )(total, upper, lower, rows)


def from_band(block, offset):
    n = lax.axis_size(BAND)
    return lax.ppermute(block, BAND, [((i + offset) % n, i) for i in range(n)])


def on_device(orbitals, rotation):
    cols = orbitals.T
    width, n = cols.shape[0], rotation.shape[1]
    sent = copies_of(rotation, lax.axis_size(GRID))
    all_rows = lax.all_to_all(sent, GRID, 0, 0, tiled=True).reshape(-1, 2, width, n)
    parity = lax.axis_index(PARITY)

    def rows(which):
        return lax.dynamic_index_in_dim(all_rows, which, 1, False).reshape(-1, n)

    same = lax.all_gather(cols, PAIRS, axis=0, tiled=True)
    upper, lower = turned(same)
    above = from_band(upper, 1)
    below = from_band(lower, -1)
    total = first_sum(upper, lower, rows(parity))
    return finished(total, above, below, rows(1 - parity))


def solution(mesh):
    n_grid, n_band = mesh.devices.shape
    fine = Mesh(
        mesh.devices.reshape(4, 4, n_grid // 16, n_band // 2, 2), (*GRID, *BAND)
    )
    spec = P(GRID, BAND)
    return jax.shard_map(
        on_device, mesh=fine, in_specs=(spec, spec), out_specs=spec, check_vma=False
    )
```

time: 159 us -> 63.8 us (0.40); the launches traced: 157 us -> 63.3 us
  waiting for transfers between devices: 137 us -> 6.11 us
  blocking collectives: 0 us -> 35 us
  starting transfers between devices: 0.04 us -> 15.7 us
  between operations: 13.4 us -> 0.07 us
  matrix products: 6.32 us -> 0 us
  Pallas kernels: 0 us -> 5.38 us
    all_gather x2 -> x0, waiting for transfers between devices: 136 us -> none  [the longest x1 76.9 us: on_device(): all_cols = lax.all_gather(orbitals, 'band', axis=1, tiled=True)]
    all_gather x0 -> x1, blocking collectives: none -> 35 us  [on_device(): same = lax.all_gather(cols, PAIRS, axis=0, tiled=True)]
    all_to_all x0 -> x1, starting transfers between devices: none -> 9.8 us  [on_device(): lax.all_to_all(sent, GRID, 0, 0, tiled=True).reshape(-1, 2, width, n)]
    dot_general x1 -> x0, matrix products: 6.32 us -> none  [on_device(): total = jnp.dot(all_cols, all_rows, preferred_element_type=jnp.float32)]
    ppermute x0 -> x2, waiting for transfers between devices: none -> 6.11 us  [from_band(): return lax.ppermute(block, BAND, [((i + offset) % n, i) for i in range(n)])]
    ppermute x0 -> x2, starting transfers between devices: none -> 5.87 us  [from_band(): return lax.ppermute(block, BAND, [((i + offset) % n, i) for i in range(n)])]
    pallas_call x0 -> x4, Pallas kernels: none -> 5.38 us  [the longest x1 2.37 us: finished(): pl.pallas_call(kernel, out_shape=jax.ShapeDtypeStruct((2 * half, n), jnp....]
  transfers between devices with their start and end apart: 2 -> 3, of which waited for: 2 -> 2; matrix products, arithmetic and copies ran while one was open for 0% -> 0% of each run, Pallas kernels for 0% -> 2%
where the time goes in v2:
time: 63.8 us; the launch traced here: 63.3 us
  blocking collectives  35 us (55%)
  starting transfers between devices  15.7 us (25%)
  waiting for transfers between devices  6.11 us (10%)
  Pallas kernels  5.38 us (8%)
  local copies, waits for them, and re-layouts  0.99 us (2%)
    all_gather x1, blocking collectives, on_device(): same = lax.all_gather(cols, PAIRS, axis=0, tiled=True)  35 us
    all_to_all x1, starting transfers between devices, on_device(): lax.all_to_all(sent, GRID, 0, 0, tiled=True).reshape(-1, 2, width, n)  9.8 us
    ppermute x2, waiting for transfers between devices, from_band(): return lax.ppermute(block, BAND, [((i + offset) % n, i) for i in range(n)])  6.11 us
    ppermute x2, starting transfers between devices, from_band(): return lax.ppermute(block, BAND, [((i + offset) % n, i) for i in range(n)])  5.87 us
    pallas_call x1, Pallas kernels, finished(): pl.pallas_call(kernel, out_shape=jax.ShapeDtypeStruct((2 * half, n), jnp....  2.37 us
    pallas_call x1, Pallas kernels, copies_of(): pl.pallas_call(kernel, out_shape=jax.ShapeDtypeStruct((n, *block.shape),...  1.56 us
  transfers between devices with their start and end apart: 3, of which 2 were waited for; matrix products, arithmetic and copies ran while one was open for 0% of the time, Pallas kernels for 2%

profile of v2, /device:TPU:6, one launch (start us, length us, event | category | flops | bytes accessed | tf_op | source)
XLA Modules:
  0.0 63.3 jit_solution(12045608183239423786)
XLA Ops:
  0.0 0.0 copy-start
  0.0 0.8 %copy-done = bf16[16,2048]{1,0:T(8,128)(2,1)S(1)} copy-done((bf16[16,2048]{1,0:T(8,128)(2,1)S(1)}, bf16[16,2048]{1,0:T(8,128)(2,1)}, u32[]{:S(2)}) %copy-start) | copy-done | bytes 65560
  0.8 1.6 %shard_map.29 = bf16[32,16,2048]{2,1,0:T(8,128)(2,1)} custom-call(bf16[16,2048]{1,0:T(8,128)(2,1)S(1)} %copy-done), custom_call_target="tpu_custom_call" | custom-call | tf_op jit(solution)/shard_map/pallas_call | solution.py:26
  2.4 0.0 copy-start.1
  2.4 9.8 %all-to-all-start = ((bf16[32,16,2048]{2,1,0:T(8,128)(2,1)}), bf16[32,16,2048]{2,1,0:T(8,128)(2,1)S(1)}, u32[]{:S(2)}, u32[]{:S(2)}) async-start(bf16[32,16,2048]{2,1,0:T(8,128)(2,1)} %shard_map.29), calls=%async_computation | async-start | bytes 4194304 | tf_op jit(solution)/shard_map/all_to_all | solution.py:129
  12.2 0.0 copy-done.1
  12.2 35.0 %all_gather.3.cols_ref = bf16[256,1024]{1,0:T(8,128)(2,1)S(1)} all-gather(bf16[32,1024]{1,0:T(8,128)(2,1)S(1)} %bitcast.11), channel_id=1, replica_groups=mesh['x'=4,'y'=4,'core'=2,'pairs'=8,'parity'=2] {'pairs'}, dimensions={0}, use_global_device_ids=true | all-gather | bytes 589824 | tf_op jit(solution)/shard_map/all_gather | solution.py:135
  47.3 0.2 shard_map.28
  47.5 4.0 %collective-permute-start = (bf16[512,256]{1,0:T(8,128)(2,1)S(1)}, bf16[512,256]{1,0:T(8,128)(2,1)S(1)}, u32[]{:S(2)}, u32[]{:S(2)}) collective-permute-start(bf16[512,256]{1,0:T(8,128)(2,1)S(1)} %get-tuple-element.7.upper_ref), channel_id=1, source_target_pairs={{1,0},{2,1},{3,2},{4,3},{5,4},{6,5},{7,6},{8,7},{9,8},{10,9},{11,1... | collective-permute-start | bytes 786440 | tf_op jit(solution)/shard_map/ppermute | solution.py:122
  51.4 1.9 %collective-permute-start.1 = (bf16[512,256]{1,0:T(8,128)(2,1)S(1)}, bf16[512,256]{1,0:T(8,128)(2,1)S(1)}, u32[]{:S(2)}, u32[]{:S(2)}) collective-permute-start(bf16[512,256]{1,0:T(8,128)(2,1)S(1)} %get-tuple-element.8.lower_ref), channel_id=1, source_target_pairs={{15,0},{0,1},{1,2},{2,3},{3,4},{4,5},{5,6},{6,7},{7,8},{8,9},{9,10... | collective-permute-start | bytes 786440 | tf_op jit(solution)/shard_map/ppermute | solution.py:122
  53.3 0.0 all-to-all-done
  53.4 0.1 constant_dynamic-slice_fusion
  53.5 1.3 %shard_map.30.total_ref = f32[1024,2048]{1,0:T(8,128)S(1)} custom-call(bf16[512,256]{1,0:T(8,128)(2,1)S(1)} %get-tuple-element.7.upper_ref, bf16[512,256]{1,0:T(8,128)(2,1)S(1)} %get-tuple-element.8.lower_ref, bf16[256,2048]{1,0:T(8,128)(2,1)S(1)} %bitcast.9), custom_call_target="tpu_custom_call" | custom-call | flops 1073741824 | bytes 8388608 | tf_op jit(solution)/shard_map/pallas_call | solution.py:67
  54.8 0.9 %collective-permute-done.upper_ref = bf16[512,256]{1,0:T(8,128)(2,1)S(1)} collective-permute-done((bf16[512,256]{1,0:T(8,128)(2,1)S(1)}, bf16[512,256]{1,0:T(8,128)(2,1)S(1)}, u32[]{:S(2)}, u32[]{:S(2)}) %collective-permute-start) | collective-permute-done | bytes 262176 | tf_op jit(solution)/shard_map/ppermute | solution.py:122
  55.7 5.2 %collective-permute-done.1.lower_ref = bf16[512,256]{1,0:T(8,128)(2,1)S(1)} collective-permute-done((bf16[512,256]{1,0:T(8,128)(2,1)S(1)}, bf16[512,256]{1,0:T(8,128)(2,1)S(1)}, u32[]{:S(2)}, u32[]{:S(2)}) %collective-permute-start.1) | collective-permute-done | bytes 262176 | tf_op jit(solution)/shard_map/ppermute | solution.py:122
  60.9 2.4 %shard_map.31 = bf16[1024,2048]{1,0:T(8,128)(2,1)} custom-call(f32[1024,2048]{1,0:T(8,128)S(1)} %shard_map.30.total_ref, bf16[512,256]{1,0:T(8,128)(2,1)S(1)} %collective-permute-done.upper_ref, bf16[512,256]{1,0:T(8,128)(2,1)S(1)} %collective-permute-done.1.lower_ref, bf16[256,2048]{1,0:T(8,128)(2,1)S(1)} %bitcast.8), custom_call_target="tpu_custom_call" | custom-call | flops 1073741824 | bytes 12582912 | tf_op jit(solution)/shard_map/pallas_call | solution.py:104
Async XLA Ops:
  0.0 0.8 %copy-start = (bf16[16,2048]{1,0:T(8,128)(2,1)S(1)}, bf16[16,2048]{1,0:T(8,128)(2,1)}, u32[]{:S(2)}) copy-start(bf16[16,2048]{1,0:T(8,128)(2,1)} %block_ref.1) | copy-start | bytes 196612
  2.4 9.8 %copy-start.1 = (bf16[1024,32]{0,1:T(8,128)(2,1)S(1)}, bf16[1024,32]{0,1:T(8,128)(2,1)}, u32[]{:S(2)}) copy-start(bf16[1024,32]{0,1:T(8,128)(2,1)} %param.2) | copy-start | bytes 196612
  2.4 51.0 %all-to-all-start = ((bf16[32,16,2048]{2,1,0:T(8,128)(2,1)}), bf16[32,16,2048]{2,1,0:T(8,128)(2,1)S(1)}, u32[]{:S(2)}, u32[]{:S(2)}) async-start(bf16[32,16,2048]{2,1,0:T(8,128)(2,1)} %shard_map.29), calls=%async_computation | async-start | bytes 4194304 | tf_op jit(solution)/shard_map/all_to_all | solution.py:129
  47.5 8.3 %collective-permute-start = (bf16[512,256]{1,0:T(8,128)(2,1)S(1)}, bf16[512,256]{1,0:T(8,128)(2,1)S(1)}, u32[]{:S(2)}, u32[]{:S(2)}) collective-permute-start(bf16[512,256]{1,0:T(8,128)(2,1)S(1)} %get-tuple-element.7.upper_ref), channel_id=1, source_target_pairs={{1,0},{2,1},{3,2},{4,3},{5,4},{6,5},{7,6},{8,7},{9,8},{10,9},{11,1... | collective-permute-start | bytes 786440 | tf_op jit(solution)/shard_map/ppermute | solution.py:122
  51.4 9.5 %collective-permute-start.1 = (bf16[512,256]{1,0:T(8,128)(2,1)S(1)}, bf16[512,256]{1,0:T(8,128)(2,1)S(1)}, u32[]{:S(2)}, u32[]{:S(2)}) collective-permute-start(bf16[512,256]{1,0:T(8,128)(2,1)S(1)} %get-tuple-element.8.lower_ref), channel_id=1, source_target_pairs={{15,0},{0,1},{1,2},{2,3},{3,4},{4,5},{5,6},{6,7},{7,8},{8,9},{9,10... | collective-permute-start | bytes 786440 | tf_op jit(solution)/shard_map/ppermute | solution.py:122

commit v3 on v2

v3 whole, which is shorter than its diff:
```python
import jax
import jax.numpy as jnp
from jax import lax
from jax.experimental import pallas as pl
from jax.experimental.pallas import tpu as pltpu
from jax.sharding import Mesh
from jax.sharding import PartitionSpec as P

GRID = ("x", "y", "core")
FAR, NEAR = "far", "near"
BAND = (FAR, NEAR)
VMEM = pl.BlockSpec(memory_space=pltpu.VMEM)
TILE = 512
CUT = 384


def params(mib):
    return pltpu.CompilerParams(vmem_limit_bytes=mib << 20)


def copies_of(block, n):
    held_n = n // 4

    def kernel(block_ref, out_ref, held, sems):
        value = block_ref[...]
        for i in range(held_n):
            held[i] = value
        copies = [
            pltpu.make_async_copy(
                held, out_ref.at[i * held_n : (i + 1) * held_n], sems.at[i]
            )
            for i in range(4)
        ]
        for copy in copies:
            copy.start()
        for copy in copies:
            copy.wait()

    return pl.pallas_call(
        kernel,
        out_shape=jax.ShapeDtypeStruct((n, *block.shape), block.dtype),
        in_specs=[VMEM],
        out_specs=pl.BlockSpec(memory_space=pltpu.HBM),
        scratch_shapes=[
            pltpu.VMEM((held_n, *block.shape), block.dtype),
            pltpu.SemaphoreType.DMA((4,)),
        ],
        compiler_params=params(4),
    )(block)


def turned(cols):
    k, points = cols.shape

    def kernel(cols_ref, out_ref):
        for i in range(0, points, 128):
            out_ref[i : i + 128, :] = cols_ref[:, i : i + 128].T

    return pl.pallas_call(
        kernel,
        out_shape=jax.ShapeDtypeStruct((points, k), cols.dtype),
        in_specs=[VMEM],
        out_specs=VMEM,
        compiler_params=params(8),
    )(cols)


def both(refs, rows, cols=slice(None), axis=1):
    return jnp.concatenate([r[rows, cols] for r in refs], axis=axis)


def first_sum(own, above, own_rows, above_rows):
    points, k = own.shape
    n = own_rows.shape[1]
    half = points // 2

    def kernel(own_ref, above_ref, own_rows_ref, above_rows_ref, sum_ref):
        for p in range(0, points, half):
            at = slice(p, p + half)
            left = both((own_ref, above_ref), at)
            for c in range(0, n, TILE):
                right = both(
                    (own_rows_ref, above_rows_ref), slice(None), slice(c, c + TILE), 0
                )
                sum_ref[at, c : c + TILE] = jnp.dot(
                    left, right, preferred_element_type=jnp.float32
                )

    return pl.pallas_call(
        kernel,
        out_shape=jax.ShapeDtypeStruct((points, n), jnp.float32),
        in_specs=[VMEM] * 4,
        out_specs=VMEM,
        compiler_params=params(12),
        cost_estimate=pl.CostEstimate(
            flops=4 * points * k * n, bytes_accessed=4 * points * n, transcendentals=0
        ),
    )(own, above, own_rows, above_rows)


def finished(total, below, upper, lower, below_rows, across_rows):
    points, k = below.shape
    n = below_rows.shape[1]
    tiles = [(h, c) for h in range(2) for c in range(0, n, TILE)]

    def kernel(
        total_ref, below_ref, upper_ref, lower_ref, below_rows_ref, across_rows_ref,
        out_ref, held, sems,
    ):
        copies = []
        for t, (h, c) in enumerate(tiles):
            at = (slice(0, CUT), slice(CUT, points))[h]
            where = (at, slice(c, c + TILE))
            left = jnp.concatenate(
                [below_ref[at, :], (upper_ref, lower_ref)[h][...]], axis=1
            )
            right = both((below_rows_ref, across_rows_ref), slice(None), where[1], 0)
            held[where] = (
                total_ref[where]
                + jnp.dot(left, right, preferred_element_type=jnp.float32)
            ).astype(jnp.bfloat16)
            copies.append(
                pltpu.make_async_copy(held.at[where], out_ref.at[where], sems.at[t])
            )
            copies[-1].start()
        for copy in copies:
            copy.wait()

    return pl.pallas_call(
        kernel,
        out_shape=jax.ShapeDtypeStruct((points, n), jnp.bfloat16),
        in_specs=[VMEM] * 6,
        out_specs=pl.BlockSpec(memory_space=pl.ANY),
        scratch_shapes=[
            pltpu.VMEM((points, n), jnp.bfloat16),
            pltpu.SemaphoreType.DMA((len(tiles),)),
        ],
        compiler_params=params(24),
        cost_estimate=pl.CostEstimate(
            flops=4 * points * k * n, bytes_accessed=6 * points * n, transcendentals=0
        ),
    )(total, below, upper, lower, below_rows, across_rows)


def from_band(block, offset):
    n = lax.axis_size(BAND)
    return lax.ppermute(block, BAND, [((i + offset) % n, i) for i in range(n)])


def on_device(orbitals, rotation):
    cols = orbitals.T
    width, n = cols.shape[0], rotation.shape[1]
    sent = copies_of(rotation, lax.axis_size(GRID))
    all_rows = lax.all_to_all(sent, GRID, 0, 0, tiled=True)
    all_rows = all_rows.reshape(-1, lax.axis_size(NEAR), width, n)
    near = lax.axis_index(NEAR)

    def rows(offset):
        which = lax.rem(near + offset, lax.axis_size(NEAR))
        return lax.dynamic_index_in_dim(all_rows, which, 1, False).reshape(-1, n)

    whole = turned(lax.all_gather(cols, FAR, axis=0, tiled=True))
    above = from_band(whole, 1)
    below = from_band(whole, -1)
    upper = from_band(above[:CUT], 1)
    lower = from_band(below[CUT:], -1)
    total = first_sum(whole, above, rows(0), rows(1))
    return finished(total, below, upper, lower, rows(3), rows(2))


def solution(mesh):
    n_grid, n_band = mesh.devices.shape
    fine = Mesh(
        mesh.devices.reshape(4, 4, n_grid // 16, n_band // 4, 4), (*GRID, *BAND)
    )
    spec = P(GRID, BAND)
    return jax.shard_map(
        on_device, mesh=fine, in_specs=(spec, spec), out_specs=spec, check_vma=False
    )
```

time: 63.8 us -> 59.1 us (0.926)
  blocking collectives: 35 us -> 25.4 us
  starting transfers between devices: 15.7 us -> 23.9 us
  waiting for transfers between devices: 6.11 us -> 3.12 us
    all_gather x1, blocking collectives: 35 us -> 25.4 us  [on_device(): whole = turned(lax.all_gather(cols, FAR, axis=0, tiled=True))]
    ppermute x2 -> x4, starting transfers between devices: 5.87 us -> 14.1 us  [from_band(): return lax.ppermute(block, BAND, [((i + offset) % n, i) for i in range(n)])]
    ppermute x2 -> x4, waiting for transfers between devices: 6.11 us -> 3.12 us  [from_band(): return lax.ppermute(block, BAND, [((i + offset) % n, i) for i in range(n)])]
  transfers between devices with their start and end apart: 3 -> 5, of which waited for: 2 -> 2; matrix products, arithmetic and copies ran while one was open for 0% -> 0% of each run, Pallas kernels for 2% -> 2%
where the time goes in v3:
time: 59.1 us; the launch traced here: 58.7 us
  blocking collectives  25.4 us (43%)
  starting transfers between devices  23.9 us (40%)
  Pallas kernels  5.1 us (9%)
  waiting for transfers between devices  3.12 us (5%)
  local copies, waits for them, and re-layouts  1.04 us (2%)
    all_gather x1, blocking collectives, on_device(): whole = turned(lax.all_gather(cols, FAR, axis=0, tiled=True))  25.4 us
    ppermute x4, starting transfers between devices, from_band(): return lax.ppermute(block, BAND, [((i + offset) % n, i) for i in range(n)])  14.1 us
    all_to_all x1, starting transfers between devices, on_device(): all_rows = lax.all_to_all(sent, GRID, 0, 0, tiled=True)  9.82 us
    ppermute x4, waiting for transfers between devices, from_band(): return lax.ppermute(block, BAND, [((i + offset) % n, i) for i in range(n)])  3.12 us
    pallas_call x1, Pallas kernels, finished(): pl.pallas_call(kernel, out_shape=jax.ShapeDtypeStruct((points, n), jnp.bf...  2.34 us
    pallas_call x1, Pallas kernels, copies_of(): pl.pallas_call(kernel, out_shape=jax.ShapeDtypeStruct((n, *block.shape),...  1.38 us
    pallas_call x1, Pallas kernels, first_sum(): pl.pallas_call(kernel, out_shape=jax.ShapeDtypeStruct((points, n), jnp.fl...  1.26 us
  transfers between devices with their start and end apart: 5, of which 2 were waited for; matrix products, arithmetic and copies ran while one was open for 0% of the time, Pallas kernels for 2%

profile of v3, /device:TPU:6, one launch (start us, length us, event | category | flops | bytes accessed | tf_op | source)
XLA Modules:
  0.0 58.7 jit_solution(574081971726224279)
XLA Ops:
  0.0 0.0 copy-start
  0.0 0.8 %copy-done = bf16[16,2048]{1,0:T(8,128)(2,1)S(1)} copy-done((bf16[16,2048]{1,0:T(8,128)(2,1)S(1)}, bf16[16,2048]{1,0:T(8,128)(2,1)}, u32[]{:S(2)}) %copy-start) | copy-done | bytes 65560
  0.8 1.4 %shard_map.29 = bf16[32,16,2048]{2,1,0:T(8,128)(2,1)} custom-call(bf16[16,2048]{1,0:T(8,128)(2,1)S(1)} %copy-done), custom_call_target="tpu_custom_call" | custom-call | tf_op jit(solution)/shard_map/pallas_call | solution.py:39
  2.2 0.0 copy-start.1
  2.2 9.8 %all-to-all-start = ((bf16[32,16,2048]{2,1,0:T(8,128)(2,1)}), bf16[32,16,2048]{2,1,0:T(8,128)(2,1)S(1)}, u32[]{:S(2)}, u32[]{:S(2)}) async-start(bf16[32,16,2048]{2,1,0:T(8,128)(2,1)} %shard_map.29), calls=%async_computation | async-start | bytes 4194304 | tf_op jit(solution)/shard_map/all_to_all | solution.py:154
  12.1 0.0 copy-done.1
  12.1 25.4 %all_gather.3.cols_ref = bf16[128,1024]{1,0:T(8,128)(2,1)S(1)} all-gather(bf16[32,1024]{1,0:T(8,128)(2,1)S(1)} %bitcast.19), channel_id=1, replica_groups=mesh['x'=4,'y'=4,'core'=2,'far'=4,'near'=4] {'far'}, dimensions={0}, use_global_device_ids=true | all-gather | bytes 327680 | tf_op jit(solution)/shard_map/all_gather | solution.py:162
  37.5 0.1 shard_map.28.own_ref
  37.6 3.4 %collective-permute-start.1 = (bf16[1024,128]{1,0:T(8,128)(2,1)S(1)}, bf16[1024,128]{1,0:T(8,128)(2,1)S(1)}, u32[]{:S(2)}, u32[]{:S(2)}) collective-permute-start(bf16[1024,128]{1,0:T(8,128)(2,1)S(1)} %shard_map.28.own_ref), channel_id=1, source_target_pairs={{15,0},{0,1},{1,2},{2,3},{3,4},{4,5},{5,6},{6,7},{7,8},{8,9},{9,10... | collective-permute-start | bytes 786440 | tf_op jit(solution)/shard_map/ppermute | solution.py:147
  41.0 3.7 %collective-permute-start = (bf16[1024,128]{1,0:T(8,128)(2,1)S(1)}, bf16[1024,128]{1,0:T(8,128)(2,1)S(1)}, u32[]{:S(2)}, u32[]{:S(2)}) collective-permute-start(bf16[1024,128]{1,0:T(8,128)(2,1)S(1)} %shard_map.28.own_ref), channel_id=1, source_target_pairs={{1,0},{2,1},{3,2},{4,3},{5,4},{6,5},{7,6},{8,7},{9,8},{10,9},{11,1... | collective-permute-start | bytes 786440 | tf_op jit(solution)/shard_map/ppermute | solution.py:147
  44.7 2.4 %collective-permute-done.1.below_ref = bf16[1024,128]{1,0:T(8,128)(2,1)S(1)} collective-permute-done((bf16[1024,128]{1,0:T(8,128)(2,1)S(1)}, bf16[1024,128]{1,0:T(8,128)(2,1)S(1)}, u32[]{:S(2)}, u32[]{:S(2)}) %collective-permute-start.1) | collective-permute-done | bytes 262176 | tf_op jit(solution)/shard_map/ppermute | solution.py:147
  47.1 2.2 %collective-permute-start.3 = (bf16[640,128]{1,0:T(8,128)(2,1)S(1)}, bf16[640,128]{1,0:T(8,128)(2,1)S(1)}, u32[]{:S(2)}, u32[]{:S(2)}) collective-permute-start(bf16[640,128]{1,0:T(8,128)(2,1)S(1)} %slice.9), channel_id=1, source_target_pairs={{15,0},{0,1},{1,2},{2,3},{3,4},{4,5},{5,6},{6,7},{7,8},{8,9},{9,10... | collective-permute-start | bytes 491528 | tf_op jit(solution)/shard_map/ppermute | solution.py:147
  49.3 0.0 collective-permute-done.above_ref
  49.3 4.9 %collective-permute-start.2 = (bf16[384,128]{1,0:T(8,128)(2,1)S(1)}, bf16[384,128]{1,0:T(8,128)(2,1)S(1)}, u32[]{:S(2)}, u32[]{:S(2)}) collective-permute-start(bf16[384,128]{1,0:T(8,128)(2,1)S(1)} %slice.8), channel_id=1, source_target_pairs={{1,0},{2,1},{3,2},{4,3},{5,4},{6,5},{7,6},{8,7},{9,8},{10,9},{11,1... | collective-permute-start | bytes 294920 | tf_op jit(solution)/shard_map/ppermute | solution.py:147
  54.2 0.0 all-to-all-done
  54.2 0.2 constant_dynamic-slice_fusion
  54.4 1.3 %shard_map.30.total_ref = f32[1024,2048]{1,0:T(8,128)S(1)} custom-call(bf16[1024,128]{1,0:T(8,128)(2,1)S(1)} %shard_map.28.own_ref, bf16[1024,128]{1,0:T(8,128)(2,1)S(1)} %collective-permute-done.above_ref, bf16[128,2048]{1,0:T(8,128)(2,1)S(1)} %bitcast.17, bf16[128,2048]{1,0:T(8,128)(2,1)S(1)} %bitcast.16), custom_call_target="tpu_custom_call" | custom-call | flops 1073741824 | bytes 8388608 | tf_op jit(solution)/shard_map/pallas_call | solution.py:89
  55.7 0.7 %collective-permute-done.2.upper_ref = bf16[384,128]{1,0:T(8,128)(2,1)S(1)} collective-permute-done((bf16[384,128]{1,0:T(8,128)(2,1)S(1)}, bf16[384,128]{1,0:T(8,128)(2,1)S(1)}, u32[]{:S(2)}, u32[]{:S(2)}) %collective-permute-start.2) | collective-permute-done | bytes 98336 | tf_op jit(solution)/shard_map/ppermute | solution.py:147
  56.4 0.0 collective-permute-done.3.lower_ref
  56.4 2.3 %shard_map.31 = bf16[1024,2048]{1,0:T(8,128)(2,1)} custom-call(f32[1024,2048]{1,0:T(8,128)S(1)} %shard_map.30.total_ref, bf16[1024,128]{1,0:T(8,128)(2,1)S(1)} %collective-permute-done.1.below_ref, bf16[384,128]{1,0:T(8,128)(2,1)S(1)} %collective-permute-done.2.upper_ref, bf16[640,128]{1,0:T(8,128)(2,1)S(1)} %collective-permute-done.3.lower_ref, ...), custom_call_target="tpu_custom_call" | custom-call | flops 1073741824 | bytes 12582912 | tf_op jit(solution)/shard_map/pallas_call | solution.py:129
  (2 shorter events, 0.0 us)
Async XLA Ops:
  0.0 0.8 %copy-start = (bf16[16,2048]{1,0:T(8,128)(2,1)S(1)}, bf16[16,2048]{1,0:T(8,128)(2,1)}, u32[]{:S(2)}) copy-start(bf16[16,2048]{1,0:T(8,128)(2,1)} %block_ref.1) | copy-start | bytes 196612
  2.2 9.8 %copy-start.1 = (bf16[1024,32]{0,1:T(8,128)(2,1)S(1)}, bf16[1024,32]{0,1:T(8,128)(2,1)}, u32[]{:S(2)}) copy-start(bf16[1024,32]{0,1:T(8,128)(2,1)} %param.2) | copy-start | bytes 196612
  2.2 52.0 %all-to-all-start = ((bf16[32,16,2048]{2,1,0:T(8,128)(2,1)}), bf16[32,16,2048]{2,1,0:T(8,128)(2,1)S(1)}, u32[]{:S(2)}, u32[]{:S(2)}) async-start(bf16[32,16,2048]{2,1,0:T(8,128)(2,1)} %shard_map.29), calls=%async_computation | async-start | bytes 4194304 | tf_op jit(solution)/shard_map/all_to_all | solution.py:154
  37.6 9.5 %collective-permute-start.1 = (bf16[1024,128]{1,0:T(8,128)(2,1)S(1)}, bf16[1024,128]{1,0:T(8,128)(2,1)S(1)}, u32[]{:S(2)}, u32[]{:S(2)}) collective-permute-start(bf16[1024,128]{1,0:T(8,128)(2,1)S(1)} %shard_map.28.own_ref), channel_id=1, source_target_pairs={{15,0},{0,1},{1,2},{2,3},{3,4},{4,5},{5,6},{6,7},{7,8},{8,9},{9,10... | collective-permute-start | bytes 786440 | tf_op jit(solution)/shard_map/ppermute | solution.py:147
  41.0 8.3 %collective-permute-start = (bf16[1024,128]{1,0:T(8,128)(2,1)S(1)}, bf16[1024,128]{1,0:T(8,128)(2,1)S(1)}, u32[]{:S(2)}, u32[]{:S(2)}) collective-permute-start(bf16[1024,128]{1,0:T(8,128)(2,1)S(1)} %shard_map.28.own_ref), channel_id=1, source_target_pairs={{1,0},{2,1},{3,2},{4,3},{5,4},{6,5},{7,6},{8,7},{9,8},{10,9},{11,1... | collective-permute-start | bytes 786440 | tf_op jit(solution)/shard_map/ppermute | solution.py:147
  47.1 9.3 %collective-permute-start.3 = (bf16[640,128]{1,0:T(8,128)(2,1)S(1)}, bf16[640,128]{1,0:T(8,128)(2,1)S(1)}, u32[]{:S(2)}, u32[]{:S(2)}) collective-permute-start(bf16[640,128]{1,0:T(8,128)(2,1)S(1)} %slice.9), channel_id=1, source_target_pairs={{15,0},{0,1},{1,2},{2,3},{3,4},{4,5},{5,6},{6,7},{7,8},{8,9},{9,10... | collective-permute-start | bytes 491528 | tf_op jit(solution)/shard_map/ppermute | solution.py:147
  49.3 7.1 %collective-permute-start.2 = (bf16[384,128]{1,0:T(8,128)(2,1)S(1)}, bf16[384,128]{1,0:T(8,128)(2,1)S(1)}, u32[]{:S(2)}, u32[]{:S(2)}) collective-permute-start(bf16[384,128]{1,0:T(8,128)(2,1)S(1)} %slice.8), channel_id=1, source_target_pairs={{1,0},{2,1},{3,2},{4,3},{5,4},{6,5},{7,6},{8,7},{9,8},{10,9},{11,1... | collective-permute-start | bytes 294920 | tf_op jit(solution)/shard_map/ppermute | solution.py:147

commit v4 on v3

--- a/solution.py
+++ b/solution.py
@@ -11,7 +11,7 @@
 BAND = (FAR, NEAR)
 VMEM = pl.BlockSpec(memory_space=pltpu.VMEM)
 TILE = 512
-CUT = 384
+CUT = 256
 
 
 def params(mib):

time: 59.1 us -> 58.8 us (level)
  no operation moved by 1% of the time
where the time goes in v4:
time: 58.8 us; the launch traced here: 58.5 us
  blocking collectives  25.4 us (43%)
  starting transfers between devices  23.9 us (41%)
  Pallas kernels  5.14 us (9%)
  waiting for transfers between devices  2.81 us (5%)
  local copies, waits for them, and re-layouts  1.04 us (2%)
    all_gather x1, blocking collectives, on_device(): whole = turned(lax.all_gather(cols, FAR, axis=0, tiled=True))  25.4 us
    ppermute x4, starting transfers between devices, from_band(): return lax.ppermute(block, BAND, [((i + offset) % n, i) for i in range(n)])  14.1 us
    all_to_all x1, starting transfers between devices, on_device(): all_rows = lax.all_to_all(sent, GRID, 0, 0, tiled=True)  9.82 us
    ppermute x4, waiting for transfers between devices, from_band(): return lax.ppermute(block, BAND, [((i + offset) % n, i) for i in range(n)])  2.81 us
    pallas_call x1, Pallas kernels, finished(): pl.pallas_call(kernel, out_shape=jax.ShapeDtypeStruct((points, n), jnp.bf...  2.37 us
    pallas_call x1, Pallas kernels, copies_of(): pl.pallas_call(kernel, out_shape=jax.ShapeDtypeStruct((n, *block.shape),...  1.38 us
    pallas_call x1, Pallas kernels, first_sum(): pl.pallas_call(kernel, out_shape=jax.ShapeDtypeStruct((points, n), jnp.fl...  1.26 us
  transfers between devices with their start and end apart: 5, of which 2 were waited for; matrix products, arithmetic and copies ran while one was open for 0% of the time, Pallas kernels for 2%

profile of v4, /device:TPU:6, one launch (start us, length us, event | category | flops | bytes accessed | tf_op | source)
XLA Modules:
  0.0 58.5 jit_solution(16348503484030405836)
XLA Ops:
  0.0 0.0 copy-start
  0.0 0.8 %copy-done = bf16[16,2048]{1,0:T(8,128)(2,1)S(1)} copy-done((bf16[16,2048]{1,0:T(8,128)(2,1)S(1)}, bf16[16,2048]{1,0:T(8,128)(2,1)}, u32[]{:S(2)}) %copy-start) | copy-done | bytes 65560
  0.8 1.4 %shard_map.29 = bf16[32,16,2048]{2,1,0:T(8,128)(2,1)} custom-call(bf16[16,2048]{1,0:T(8,128)(2,1)S(1)} %copy-done), custom_call_target="tpu_custom_call" | custom-call | tf_op jit(solution)/shard_map/pallas_call | solution.py:39
  2.2 0.0 copy-start.1
  2.2 9.8 %all-to-all-start = ((bf16[32,16,2048]{2,1,0:T(8,128)(2,1)}), bf16[32,16,2048]{2,1,0:T(8,128)(2,1)S(1)}, u32[]{:S(2)}, u32[]{:S(2)}) async-start(bf16[32,16,2048]{2,1,0:T(8,128)(2,1)} %shard_map.29), calls=%async_computation | async-start | bytes 4194304 | tf_op jit(solution)/shard_map/all_to_all | solution.py:154
  12.1 0.0 copy-done.1
  12.1 25.4 %all_gather.3.cols_ref = bf16[128,1024]{1,0:T(8,128)(2,1)S(1)} all-gather(bf16[32,1024]{1,0:T(8,128)(2,1)S(1)} %bitcast.19), channel_id=1, replica_groups=mesh['x'=4,'y'=4,'core'=2,'far'=4,'near'=4] {'far'}, dimensions={0}, use_global_device_ids=true | all-gather | bytes 327680 | tf_op jit(solution)/shard_map/all_gather | solution.py:162
  37.5 0.1 shard_map.28.own_ref
  37.6 3.4 %collective-permute-start.1 = (bf16[1024,128]{1,0:T(8,128)(2,1)S(1)}, bf16[1024,128]{1,0:T(8,128)(2,1)S(1)}, u32[]{:S(2)}, u32[]{:S(2)}) collective-permute-start(bf16[1024,128]{1,0:T(8,128)(2,1)S(1)} %shard_map.28.own_ref), channel_id=1, source_target_pairs={{15,0},{0,1},{1,2},{2,3},{3,4},{4,5},{5,6},{6,7},{7,8},{8,9},{9,10... | collective-permute-start | bytes 786440 | tf_op jit(solution)/shard_map/ppermute | solution.py:147
  41.0 3.7 %collective-permute-start = (bf16[1024,128]{1,0:T(8,128)(2,1)S(1)}, bf16[1024,128]{1,0:T(8,128)(2,1)S(1)}, u32[]{:S(2)}, u32[]{:S(2)}) collective-permute-start(bf16[1024,128]{1,0:T(8,128)(2,1)S(1)} %shard_map.28.own_ref), channel_id=1, source_target_pairs={{1,0},{2,1},{3,2},{4,3},{5,4},{6,5},{7,6},{8,7},{9,8},{10,9},{11,1... | collective-permute-start | bytes 786440 | tf_op jit(solution)/shard_map/ppermute | solution.py:147
  44.7 2.4 %collective-permute-done.1.below_ref = bf16[1024,128]{1,0:T(8,128)(2,1)S(1)} collective-permute-done((bf16[1024,128]{1,0:T(8,128)(2,1)S(1)}, bf16[1024,128]{1,0:T(8,128)(2,1)S(1)}, u32[]{:S(2)}, u32[]{:S(2)}) %collective-permute-start.1) | collective-permute-done | bytes 262176 | tf_op jit(solution)/shard_map/ppermute | solution.py:147
  47.1 2.2 %collective-permute-start.3 = (bf16[768,128]{1,0:T(8,128)(2,1)S(1)}, bf16[768,128]{1,0:T(8,128)(2,1)S(1)}, u32[]{:S(2)}, u32[]{:S(2)}) collective-permute-start(bf16[768,128]{1,0:T(8,128)(2,1)S(1)} %slice.9), channel_id=1, source_target_pairs={{15,0},{0,1},{1,2},{2,3},{3,4},{4,5},{5,6},{6,7},{7,8},{8,9},{9,10... | collective-permute-start | bytes 589832 | tf_op jit(solution)/shard_map/ppermute | solution.py:147
  49.3 0.0 collective-permute-done.above_ref
  49.3 4.9 %collective-permute-start.2 = (bf16[256,128]{1,0:T(8,128)(2,1)S(1)}, bf16[256,128]{1,0:T(8,128)(2,1)S(1)}, u32[]{:S(2)}, u32[]{:S(2)}) collective-permute-start(bf16[256,128]{1,0:T(8,128)(2,1)S(1)} %slice.8), channel_id=1, source_target_pairs={{1,0},{2,1},{3,2},{4,3},{5,4},{6,5},{7,6},{8,7},{9,8},{10,9},{11,1... | collective-permute-start | bytes 196616 | tf_op jit(solution)/shard_map/ppermute | solution.py:147
  54.2 0.0 all-to-all-done
  54.2 0.2 constant_dynamic-slice_fusion
  54.4 1.3 %shard_map.30.total_ref = f32[1024,2048]{1,0:T(8,128)S(1)} custom-call(bf16[1024,128]{1,0:T(8,128)(2,1)S(1)} %shard_map.28.own_ref, bf16[1024,128]{1,0:T(8,128)(2,1)S(1)} %collective-permute-done.above_ref, bf16[128,2048]{1,0:T(8,128)(2,1)S(1)} %bitcast.17, bf16[128,2048]{1,0:T(8,128)(2,1)S(1)} %bitcast.16), custom_call_target="tpu_custom_call" | custom-call | flops 1073741824 | bytes 8388608 | tf_op jit(solution)/shard_map/pallas_call | solution.py:89
  55.7 0.4 collective-permute-done.2.upper_ref
  56.1 0.0 collective-permute-done.3.lower_ref
  56.1 2.4 %shard_map.31 = bf16[1024,2048]{1,0:T(8,128)(2,1)} custom-call(f32[1024,2048]{1,0:T(8,128)S(1)} %shard_map.30.total_ref, bf16[1024,128]{1,0:T(8,128)(2,1)S(1)} %collective-permute-done.1.below_ref, bf16[256,128]{1,0:T(8,128)(2,1)S(1)} %collective-permute-done.2.upper_ref, bf16[768,128]{1,0:T(8,128)(2,1)S(1)} %collective-permute-done.3.lower_ref, ...), custom_call_target="tpu_custom_call" | custom-call | flops 1073741824 | bytes 12582912 | tf_op jit(solution)/shard_map/pallas_call | solution.py:129
  (2 shorter events, 0.0 us)
Async XLA Ops:
  0.0 0.8 %copy-start = (bf16[16,2048]{1,0:T(8,128)(2,1)S(1)}, bf16[16,2048]{1,0:T(8,128)(2,1)}, u32[]{:S(2)}) copy-start(bf16[16,2048]{1,0:T(8,128)(2,1)} %block_ref.1) | copy-start | bytes 196612
  2.2 9.8 %copy-start.1 = (bf16[1024,32]{0,1:T(8,128)(2,1)S(1)}, bf16[1024,32]{0,1:T(8,128)(2,1)}, u32[]{:S(2)}) copy-start(bf16[1024,32]{0,1:T(8,128)(2,1)} %param.2) | copy-start | bytes 196612
  2.2 52.0 %all-to-all-start = ((bf16[32,16,2048]{2,1,0:T(8,128)(2,1)}), bf16[32,16,2048]{2,1,0:T(8,128)(2,1)S(1)}, u32[]{:S(2)}, u32[]{:S(2)}) async-start(bf16[32,16,2048]{2,1,0:T(8,128)(2,1)} %shard_map.29), calls=%async_computation | async-start | bytes 4194304 | tf_op jit(solution)/shard_map/all_to_all | solution.py:154
  37.6 9.5 %collective-permute-start.1 = (bf16[1024,128]{1,0:T(8,128)(2,1)S(1)}, bf16[1024,128]{1,0:T(8,128)(2,1)S(1)}, u32[]{:S(2)}, u32[]{:S(2)}) collective-permute-start(bf16[1024,128]{1,0:T(8,128)(2,1)S(1)} %shard_map.28.own_ref), channel_id=1, source_target_pairs={{15,0},{0,1},{1,2},{2,3},{3,4},{4,5},{5,6},{6,7},{7,8},{8,9},{9,10... | collective-permute-start | bytes 786440 | tf_op jit(solution)/shard_map/ppermute | solution.py:147
  41.0 8.3 %collective-permute-start = (bf16[1024,128]{1,0:T(8,128)(2,1)S(1)}, bf16[1024,128]{1,0:T(8,128)(2,1)S(1)}, u32[]{:S(2)}, u32[]{:S(2)}) collective-permute-start(bf16[1024,128]{1,0:T(8,128)(2,1)S(1)} %shard_map.28.own_ref), channel_id=1, source_target_pairs={{1,0},{2,1},{3,2},{4,3},{5,4},{6,5},{7,6},{8,7},{9,8},{10,9},{11,1... | collective-permute-start | bytes 786440 | tf_op jit(solution)/shard_map/ppermute | solution.py:147
  47.1 9.0 %collective-permute-start.3 = (bf16[768,128]{1,0:T(8,128)(2,1)S(1)}, bf16[768,128]{1,0:T(8,128)(2,1)S(1)}, u32[]{:S(2)}, u32[]{:S(2)}) collective-permute-start(bf16[768,128]{1,0:T(8,128)(2,1)S(1)} %slice.9), channel_id=1, source_target_pairs={{15,0},{0,1},{1,2},{2,3},{3,4},{4,5},{5,6},{6,7},{7,8},{8,9},{9,10... | collective-permute-start | bytes 589832 | tf_op jit(solution)/shard_map/ppermute | solution.py:147
  49.3 6.8 %collective-permute-start.2 = (bf16[256,128]{1,0:T(8,128)(2,1)S(1)}, bf16[256,128]{1,0:T(8,128)(2,1)S(1)}, u32[]{:S(2)}, u32[]{:S(2)}) collective-permute-start(bf16[256,128]{1,0:T(8,128)(2,1)S(1)} %slice.8), channel_id=1, source_target_pairs={{1,0},{2,1},{3,2},{4,3},{5,4},{6,5},{7,6},{8,7},{9,8},{10,9},{11,1... | collective-permute-start | bytes 196616 | tf_op jit(solution)/shard_map/ppermute | solution.py:147

commit v5 on v4

--- a/solution.py
+++ b/solution.py
@@ -11,7 +11,7 @@
 BAND = (FAR, NEAR)
 VMEM = pl.BlockSpec(memory_space=pltpu.VMEM)
 TILE = 512
-CUT = 256
+CUT = 512
 
 
 def params(mib):
@@ -98,22 +98,20 @@
     )(own, above, own_rows, above_rows)
 
 
-def finished(total, below, upper, lower, below_rows, across_rows):
+def finished(total, below, across, below_rows, across_rows):
     points, k = below.shape
     n = below_rows.shape[1]
     tiles = [(h, c) for h in range(2) for c in range(0, n, TILE)]
 
     def kernel(
-        total_ref, below_ref, upper_ref, lower_ref, below_rows_ref, across_rows_ref,
+        total_ref, below_ref, across_ref, below_rows_ref, across_rows_ref,
         out_ref, held, sems,
     ):
         copies = []
         for t, (h, c) in enumerate(tiles):
             at = (slice(0, CUT), slice(CUT, points))[h]
             where = (at, slice(c, c + TILE))
-            left = jnp.concatenate(
-                [below_ref[at, :], (upper_ref, lower_ref)[h][...]], axis=1
-            )
+            left = both((below_ref, across_ref), at)
             right = both((below_rows_ref, across_rows_ref), slice(None), where[1], 0)
             held[where] = (
                 total_ref[where]
@@ -129,7 +127,7 @@
     return pl.pallas_call(
         kernel,
         out_shape=jax.ShapeDtypeStruct((points, n), jnp.bfloat16),
-        in_specs=[VMEM] * 6,
+        in_specs=[VMEM] * 5,
         out_specs=pl.BlockSpec(memory_space=pl.ANY),
         scratch_shapes=[
             pltpu.VMEM((points, n), jnp.bfloat16),
@@ -139,7 +137,7 @@
         cost_estimate=pl.CostEstimate(
             flops=4 * points * k * n, bytes_accessed=6 * points * n, transcendentals=0
         ),
-    )(total, below, upper, lower, below_rows, across_rows)
+    )(total, below, across, below_rows, across_rows)
 
 
 def from_band(block, offset):
@@ -162,10 +160,9 @@
     whole = turned(lax.all_gather(cols, FAR, axis=0, tiled=True))
     above = from_band(whole, 1)
     below = from_band(whole, -1)
-    upper = from_band(above[:CUT], 1)
-    lower = from_band(below[CUT:], -1)
-    total = first_sum(whole, above, rows(0), rows(1))
-    return finished(total, below, upper, lower, rows(3), rows(2))
+    across = from_band(above, 1)
+    total = first_sum(whole, below, rows(0), rows(3))
+    return finished(total, above, across, rows(1), rows(2))
 
 
 def solution(mesh):

time: 58.8 us -> 58.1 us (0.988)
  starting transfers between devices: 23.9 us -> 21.1 us
  waiting for transfers between devices: 2.81 us -> 4.61 us
    ppermute x4 -> x3, starting transfers between devices: 14.1 us -> 11.3 us  [from_band(): return lax.ppermute(block, BAND, [((i + offset) % n, i) for i in range(n)])]
    ppermute x4 -> x3, waiting for transfers between devices: 2.81 us -> 4.61 us  [from_band(): return lax.ppermute(block, BAND, [((i + offset) % n, i) for i in range(n)])]
  transfers between devices with their start and end apart: 5 -> 4, of which waited for: 2 -> 2; matrix products, arithmetic and copies ran while one was open for 0% -> 0% of each run, Pallas kernels for 2% -> 2%
where the time goes in v5:
time: 58.1 us; the launch traced here: 57.4 us
  blocking collectives  25.4 us (44%)
  starting transfers between devices  21.1 us (36%)
  Pallas kernels  5.13 us (9%)
  waiting for transfers between devices  4.61 us (8%)
  local copies, waits for them, and re-layouts  1.02 us (2%)
    all_gather x1, blocking collectives, on_device(): whole = turned(lax.all_gather(cols, FAR, axis=0, tiled=True))  25.4 us
    ppermute x3, starting transfers between devices, from_band(): return lax.ppermute(block, BAND, [((i + offset) % n, i) for i in range(n)])  11.3 us
    all_to_all x1, starting transfers between devices, on_device(): all_rows = lax.all_to_all(sent, GRID, 0, 0, tiled=True)  9.82 us
    ppermute x3, waiting for transfers between devices, from_band(): return lax.ppermute(block, BAND, [((i + offset) % n, i) for i in range(n)])  4.61 us
    pallas_call x1, Pallas kernels, finished(): pl.pallas_call(kernel, out_shape=jax.ShapeDtypeStruct((points, n), jnp.bf...  2.37 us
    pallas_call x1, Pallas kernels, copies_of(): pl.pallas_call(kernel, out_shape=jax.ShapeDtypeStruct((n, *block.shape),...  1.38 us
    pallas_call x1, Pallas kernels, first_sum(): pl.pallas_call(kernel, out_shape=jax.ShapeDtypeStruct((points, n), jnp.fl...  1.26 us
  transfers between devices with their start and end apart: 4, of which 2 were waited for; matrix products, arithmetic and copies ran while one was open for 0% of the time, Pallas kernels for 2%

profile of v5, /device:TPU:6, one launch (start us, length us, event | category | flops | bytes accessed | tf_op | source)
XLA Modules:
  0.0 57.4 jit_solution(15441547444296204996)
XLA Ops:
  0.0 0.0 copy-start
  0.0 0.8 %copy-done = bf16[16,2048]{1,0:T(8,128)(2,1)S(1)} copy-done((bf16[16,2048]{1,0:T(8,128)(2,1)S(1)}, bf16[16,2048]{1,0:T(8,128)(2,1)}, u32[]{:S(2)}) %copy-start) | copy-done | bytes 65560
  0.8 1.4 %shard_map.29 = bf16[32,16,2048]{2,1,0:T(8,128)(2,1)} custom-call(bf16[16,2048]{1,0:T(8,128)(2,1)S(1)} %copy-done), custom_call_target="tpu_custom_call" | custom-call | tf_op jit(solution)/shard_map/pallas_call | solution.py:39
  2.2 0.0 copy-start.1
  2.2 9.8 %all-to-all-start = ((bf16[32,16,2048]{2,1,0:T(8,128)(2,1)}), bf16[32,16,2048]{2,1,0:T(8,128)(2,1)S(1)}, u32[]{:S(2)}, u32[]{:S(2)}) async-start(bf16[32,16,2048]{2,1,0:T(8,128)(2,1)} %shard_map.29), calls=%async_computation | async-start | bytes 4194304 | tf_op jit(solution)/shard_map/all_to_all | solution.py:152
  12.1 0.0 copy-done.1
  12.1 25.4 %all_gather.3.cols_ref = bf16[128,1024]{1,0:T(8,128)(2,1)S(1)} all-gather(bf16[32,1024]{1,0:T(8,128)(2,1)S(1)} %bitcast.19), channel_id=1, replica_groups=mesh['x'=4,'y'=4,'core'=2,'far'=4,'near'=4] {'far'}, dimensions={0}, use_global_device_ids=true | all-gather | bytes 327680 | tf_op jit(solution)/shard_map/all_gather | solution.py:160
  37.5 0.1 shard_map.28.own_ref
  37.6 4.1 %collective-permute-start.1 = (bf16[1024,128]{1,0:T(8,128)(2,1)S(1)}, bf16[1024,128]{1,0:T(8,128)(2,1)S(1)}, u32[]{:S(2)}, u32[]{:S(2)}) collective-permute-start(bf16[1024,128]{1,0:T(8,128)(2,1)S(1)} %shard_map.28.own_ref), channel_id=1, source_target_pairs={{1,0},{2,1},{3,2},{4,3},{5,4},{6,5},{7,6},{8,7},{9,8},{10,9},{11,1... | collective-permute-start | bytes 786440 | tf_op jit(solution)/shard_map/ppermute | solution.py:145
  41.7 1.9 %collective-permute-start = (bf16[1024,128]{1,0:T(8,128)(2,1)S(1)}, bf16[1024,128]{1,0:T(8,128)(2,1)S(1)}, u32[]{:S(2)}, u32[]{:S(2)}) collective-permute-start(bf16[1024,128]{1,0:T(8,128)(2,1)S(1)} %shard_map.28.own_ref), channel_id=1, source_target_pairs={{15,0},{0,1},{1,2},{2,3},{3,4},{4,5},{5,6},{6,7},{7,8},{8,9},{9,10... | collective-permute-start | bytes 786440 | tf_op jit(solution)/shard_map/ppermute | solution.py:145
  43.7 2.2 %collective-permute-done.1.below_ref = bf16[1024,128]{1,0:T(8,128)(2,1)S(1)} collective-permute-done((bf16[1024,128]{1,0:T(8,128)(2,1)S(1)}, bf16[1024,128]{1,0:T(8,128)(2,1)S(1)}, u32[]{:S(2)}, u32[]{:S(2)}) %collective-permute-start.1) | collective-permute-done | bytes 262176 | tf_op jit(solution)/shard_map/ppermute | solution.py:145
  45.9 5.3 %collective-permute-start.2 = (bf16[1024,128]{1,0:T(8,128)(2,1)S(1)}, bf16[1024,128]{1,0:T(8,128)(2,1)S(1)}, u32[]{:S(2)}, u32[]{:S(2)}) collective-permute-start(bf16[1024,128]{1,0:T(8,128)(2,1)S(1)} %collective-permute-done.1.below_ref), channel_id=1, source_target_pairs={{1,0},{2,1},{3,2},{4,3},{5,4},{6,5},{7,6},{8,7},{9,8},{10,9},{11,1... | collective-permute-start | bytes 786440 | tf_op jit(solution)/shard_map/ppermute | solution.py:145
  51.2 0.0 all-to-all-done
  51.2 0.2 constant_dynamic-slice_fusion
  51.4 0.0 collective-permute-done.above_ref
  51.4 1.3 %shard_map.30.total_ref = f32[1024,2048]{1,0:T(8,128)S(1)} custom-call(bf16[1024,128]{1,0:T(8,128)(2,1)S(1)} %shard_map.28.own_ref, bf16[1024,128]{1,0:T(8,128)(2,1)S(1)} %collective-permute-done.above_ref, bf16[128,2048]{1,0:T(8,128)(2,1)S(1)} %bitcast.17, bf16[128,2048]{1,0:T(8,128)(2,1)S(1)} %bitcast.16), custom_call_target="tpu_custom_call" | custom-call | flops 1073741824 | bytes 8388608 | tf_op jit(solution)/shard_map/pallas_call | solution.py:89
  52.6 2.4 %collective-permute-done.2.across_ref = bf16[1024,128]{1,0:T(8,128)(2,1)S(1)} collective-permute-done((bf16[1024,128]{1,0:T(8,128)(2,1)S(1)}, bf16[1024,128]{1,0:T(8,128)(2,1)S(1)}, u32[]{:S(2)}, u32[]{:S(2)}) %collective-permute-start.2) | collective-permute-done | bytes 262176 | tf_op jit(solution)/shard_map/ppermute | solution.py:145
  55.0 2.4 %shard_map.31 = bf16[1024,2048]{1,0:T(8,128)(2,1)} custom-call(f32[1024,2048]{1,0:T(8,128)S(1)} %shard_map.30.total_ref, bf16[1024,128]{1,0:T(8,128)(2,1)S(1)} %collective-permute-done.1.below_ref, bf16[1024,128]{1,0:T(8,128)(2,1)S(1)} %collective-permute-done.2.across_ref, bf16[128,2048]{1,0:T(8,128)(2,1)S(1)} %bitcast.15, bf16[128,2048]{1,0:T(8,128)(2,1)S(1)} %bitcast.14), custom_call_target="tpu_custom_call" | custom-call | flops 1073741824 | bytes 12582912 | tf_op jit(solution)/shard_map/pallas_call | solution.py:127
Async XLA Ops:
  0.0 0.8 %copy-start = (bf16[16,2048]{1,0:T(8,128)(2,1)S(1)}, bf16[16,2048]{1,0:T(8,128)(2,1)}, u32[]{:S(2)}) copy-start(bf16[16,2048]{1,0:T(8,128)(2,1)} %block_ref.1) | copy-start | bytes 196612
  2.2 9.8 %copy-start.1 = (bf16[1024,32]{0,1:T(8,128)(2,1)S(1)}, bf16[1024,32]{0,1:T(8,128)(2,1)}, u32[]{:S(2)}) copy-start(bf16[1024,32]{0,1:T(8,128)(2,1)} %param.2) | copy-start | bytes 196612
  2.2 48.9 %all-to-all-start = ((bf16[32,16,2048]{2,1,0:T(8,128)(2,1)}), bf16[32,16,2048]{2,1,0:T(8,128)(2,1)S(1)}, u32[]{:S(2)}, u32[]{:S(2)}) async-start(bf16[32,16,2048]{2,1,0:T(8,128)(2,1)} %shard_map.29), calls=%async_computation | async-start | bytes 4194304 | tf_op jit(solution)/shard_map/all_to_all | solution.py:152
  37.6 8.3 %collective-permute-start.1 = (bf16[1024,128]{1,0:T(8,128)(2,1)S(1)}, bf16[1024,128]{1,0:T(8,128)(2,1)S(1)}, u32[]{:S(2)}, u32[]{:S(2)}) collective-permute-start(bf16[1024,128]{1,0:T(8,128)(2,1)S(1)} %shard_map.28.own_ref), channel_id=1, source_target_pairs={{1,0},{2,1},{3,2},{4,3},{5,4},{6,5},{7,6},{8,7},{9,8},{10,9},{11,1... | collective-permute-start | bytes 786440 | tf_op jit(solution)/shard_map/ppermute | solution.py:145
  41.7 9.7 %collective-permute-start = (bf16[1024,128]{1,0:T(8,128)(2,1)S(1)}, bf16[1024,128]{1,0:T(8,128)(2,1)S(1)}, u32[]{:S(2)}, u32[]{:S(2)}) collective-permute-start(bf16[1024,128]{1,0:T(8,128)(2,1)S(1)} %shard_map.28.own_ref), channel_id=1, source_target_pairs={{15,0},{0,1},{1,2},{2,3},{3,4},{4,5},{5,6},{6,7},{7,8},{8,9},{9,10... | collective-permute-start | bytes 786440 | tf_op jit(solution)/shard_map/ppermute | solution.py:145
  45.9 9.2 %collective-permute-start.2 = (bf16[1024,128]{1,0:T(8,128)(2,1)S(1)}, bf16[1024,128]{1,0:T(8,128)(2,1)S(1)}, u32[]{:S(2)}, u32[]{:S(2)}) collective-permute-start(bf16[1024,128]{1,0:T(8,128)(2,1)S(1)} %collective-permute-done.1.below_ref), channel_id=1, source_target_pairs={{1,0},{2,1},{3,2},{4,3},{5,4},{6,5},{7,6},{8,7},{9,8},{10,9},{11,1... | collective-permute-start | bytes 786440 | tf_op jit(solution)/shard_map/ppermute | solution.py:145

commit v6 on v5

--- a/solution.py
+++ b/solution.py
@@ -69,19 +69,18 @@
     return jnp.concatenate([r[rows, cols] for r in refs], axis=axis)
 
 
-def first_sum(own, above, own_rows, above_rows):
-    points, k = own.shape
-    n = own_rows.shape[1]
+def first_sum(parts, rows):
+    points, k = parts[0].shape
+    n, count = rows[0].shape[1], len(parts)
     half = points // 2
 
-    def kernel(own_ref, above_ref, own_rows_ref, above_rows_ref, sum_ref):
+    def kernel(*refs):
+        parts_refs, rows_refs, sum_ref = refs[:count], refs[count:-1], refs[-1]
         for p in range(0, points, half):
             at = slice(p, p + half)
-            left = both((own_ref, above_ref), at)
+            left = both(parts_refs, at)
             for c in range(0, n, TILE):
-                right = both(
-                    (own_rows_ref, above_rows_ref), slice(None), slice(c, c + TILE), 0
-                )
+                right = both(rows_refs, slice(None), slice(c, c + TILE), 0)
                 sum_ref[at, c : c + TILE] = jnp.dot(
                     left, right, preferred_element_type=jnp.float32
                 )
@@ -89,30 +88,29 @@
     return pl.pallas_call(
         kernel,
         out_shape=jax.ShapeDtypeStruct((points, n), jnp.float32),
-        in_specs=[VMEM] * 4,
+        in_specs=[VMEM] * (2 * count),
         out_specs=VMEM,
         compiler_params=params(12),
         cost_estimate=pl.CostEstimate(
-            flops=4 * points * k * n, bytes_accessed=4 * points * n, transcendentals=0
+            flops=6 * points * k * n, bytes_accessed=4 * points * n, transcendentals=0
         ),
-    )(own, above, own_rows, above_rows)
+    )(*parts, *rows)
 
 
-def finished(total, below, across, below_rows, across_rows):
-    points, k = below.shape
-    n = below_rows.shape[1]
+def finished(total, across, across_rows):
+    points, k = across.shape
+    n = across_rows.shape[1]
     tiles = [(h, c) for h in range(2) for c in range(0, n, TILE)]
 
     def kernel(
-        total_ref, below_ref, across_ref, below_rows_ref, across_rows_ref,
-        out_ref, held, sems,
+        total_ref, across_ref, across_rows_ref, out_ref, held, sems
     ):
         copies = []
         for t, (h, c) in enumerate(tiles):
             at = (slice(0, CUT), slice(CUT, points))[h]
             where = (at, slice(c, c + TILE))
-            left = both((below_ref, across_ref), at)
-            right = both((below_rows_ref, across_rows_ref), slice(None), where[1], 0)
+            left = across_ref[at, :]
+            right = across_rows_ref[:, where[1]]
             held[where] = (
                 total_ref[where]
                 + jnp.dot(left, right, preferred_element_type=jnp.float32)
@@ -127,7 +125,7 @@
     return pl.pallas_call(
         kernel,
         out_shape=jax.ShapeDtypeStruct((points, n), jnp.bfloat16),
-        in_specs=[VMEM] * 5,
+        in_specs=[VMEM] * 3,
         out_specs=pl.BlockSpec(memory_space=pl.ANY),
         scratch_shapes=[
             pltpu.VMEM((points, n), jnp.bfloat16),
@@ -137,7 +135,7 @@
         cost_estimate=pl.CostEstimate(
             flops=4 * points * k * n, bytes_accessed=6 * points * n, transcendentals=0
         ),
-    )(total, below, across, below_rows, across_rows)
+    )(total, across, across_rows)
 
 
 def from_band(block, offset):
@@ -161,8 +159,8 @@
     above = from_band(whole, 1)
     below = from_band(whole, -1)
     across = from_band(above, 1)
-    total = first_sum(whole, below, rows(0), rows(3))
-    return finished(total, above, across, rows(1), rows(2))
+    total = first_sum((whole, below, above), (rows(0), rows(3), rows(1)))
+    return finished(total, across, rows(2))
 
 
 def solution(mesh):

time: 58.1 us -> 58.1 us (level)
  waiting for transfers between devices: 4.61 us -> 3.48 us
  Pallas kernels: 5.13 us -> 6.21 us
    ppermute x3, waiting for transfers between devices: 4.61 us -> 3.48 us  [from_band(): return lax.ppermute(block, BAND, [((i + offset) % n, i) for i in range(n)])]
    pallas_call x1, Pallas kernels: 1.26 us -> 2.35 us  [first_sum(): pl.pallas_call(kernel, out_shape=jax.ShapeDtypeStruct((points, n), jnp.fl...]
  transfers between devices with their start and end apart: 4 -> 4, of which waited for: 2 -> 2; matrix products, arithmetic and copies ran while one was open for 0% -> 0% of each run, Pallas kernels for 2% -> 4%
where the time goes in v6:
time: 58.1 us; the launch traced here: 57.4 us
  blocking collectives  25.4 us (44%)
  starting transfers between devices  21.1 us (36%)
  Pallas kernels  6.21 us (11%)
  waiting for transfers between devices  3.48 us (6%)
  local copies, waits for them, and re-layouts  1.06 us (2%)
    all_gather x1, blocking collectives, on_device(): whole = turned(lax.all_gather(cols, FAR, axis=0, tiled=True))  25.4 us
    ppermute x3, starting transfers between devices, from_band(): return lax.ppermute(block, BAND, [((i + offset) % n, i) for i in range(n)])  11.3 us
    all_to_all x1, starting transfers between devices, on_device(): all_rows = lax.all_to_all(sent, GRID, 0, 0, tiled=True)  9.82 us
    ppermute x3, waiting for transfers between devices, from_band(): return lax.ppermute(block, BAND, [((i + offset) % n, i) for i in range(n)])  3.48 us
    pallas_call x1, Pallas kernels, finished(): pl.pallas_call(kernel, out_shape=jax.ShapeDtypeStruct((points, n), jnp.bf...  2.36 us
    pallas_call x1, Pallas kernels, first_sum(): pl.pallas_call(kernel, out_shape=jax.ShapeDtypeStruct((points, n), jnp.fl...  2.35 us
    pallas_call x1, Pallas kernels, copies_of(): pl.pallas_call(kernel, out_shape=jax.ShapeDtypeStruct((n, *block.shape),...  1.38 us
  transfers between devices with their start and end apart: 4, of which 2 were waited for; matrix products, arithmetic and copies ran while one was open for 0% of the time, Pallas kernels for 4%

profile of v6, /device:TPU:6, one launch (start us, length us, event | category | flops | bytes accessed | tf_op | source)
XLA Modules:
  0.0 57.4 jit_solution(16163223223333087603)
XLA Ops:
  0.0 0.0 copy-start
  0.0 0.8 %copy-done = bf16[16,2048]{1,0:T(8,128)(2,1)S(1)} copy-done((bf16[16,2048]{1,0:T(8,128)(2,1)S(1)}, bf16[16,2048]{1,0:T(8,128)(2,1)}, u32[]{:S(2)}) %copy-start) | copy-done | bytes 65560
  0.8 1.4 %shard_map.29 = bf16[32,16,2048]{2,1,0:T(8,128)(2,1)} custom-call(bf16[16,2048]{1,0:T(8,128)(2,1)S(1)} %copy-done), custom_call_target="tpu_custom_call" | custom-call | tf_op jit(solution)/shard_map/pallas_call | solution.py:39
  2.2 0.0 copy-start.1
  2.2 9.8 %all-to-all-start = ((bf16[32,16,2048]{2,1,0:T(8,128)(2,1)}), bf16[32,16,2048]{2,1,0:T(8,128)(2,1)S(1)}, u32[]{:S(2)}, u32[]{:S(2)}) async-start(bf16[32,16,2048]{2,1,0:T(8,128)(2,1)} %shard_map.29), calls=%async_computation | async-start | bytes 4194304 | tf_op jit(solution)/shard_map/all_to_all | solution.py:150
  12.1 0.0 copy-done.1
  12.1 25.4 %all_gather.3.cols_ref = bf16[128,1024]{1,0:T(8,128)(2,1)S(1)} all-gather(bf16[32,1024]{1,0:T(8,128)(2,1)S(1)} %bitcast.19), channel_id=1, replica_groups=mesh['x'=4,'y'=4,'core'=2,'far'=4,'near'=4] {'far'}, dimensions={0}, use_global_device_ids=true | all-gather | bytes 327680 | tf_op jit(solution)/shard_map/all_gather | solution.py:158
  37.5 0.1 shard_map.28.refs_0_
  37.6 4.1 %collective-permute-start.1 = (bf16[1024,128]{1,0:T(8,128)(2,1)S(1)}, bf16[1024,128]{1,0:T(8,128)(2,1)S(1)}, u32[]{:S(2)}, u32[]{:S(2)}) collective-permute-start(bf16[1024,128]{1,0:T(8,128)(2,1)S(1)} %shard_map.28.refs_0_), channel_id=1, source_target_pairs={{1,0},{2,1},{3,2},{4,3},{5,4},{6,5},{7,6},{8,7},{9,8},{10,9},{11,1... | collective-permute-start | bytes 786440 | tf_op jit(solution)/shard_map/ppermute | solution.py:143
  41.7 1.9 %collective-permute-start = (bf16[1024,128]{1,0:T(8,128)(2,1)S(1)}, bf16[1024,128]{1,0:T(8,128)(2,1)S(1)}, u32[]{:S(2)}, u32[]{:S(2)}) collective-permute-start(bf16[1024,128]{1,0:T(8,128)(2,1)S(1)} %shard_map.28.refs_0_), channel_id=1, source_target_pairs={{15,0},{0,1},{1,2},{2,3},{3,4},{4,5},{5,6},{6,7},{7,8},{8,9},{9,10... | collective-permute-start | bytes 786440 | tf_op jit(solution)/shard_map/ppermute | solution.py:143
  43.7 2.2 %collective-permute-done.1.refs_2_ = bf16[1024,128]{1,0:T(8,128)(2,1)S(1)} collective-permute-done((bf16[1024,128]{1,0:T(8,128)(2,1)S(1)}, bf16[1024,128]{1,0:T(8,128)(2,1)S(1)}, u32[]{:S(2)}, u32[]{:S(2)}) %collective-permute-start.1) | collective-permute-done | bytes 262176 | tf_op jit(solution)/shard_map/ppermute | solution.py:143
  45.9 5.3 %collective-permute-start.2 = (bf16[1024,128]{1,0:T(8,128)(2,1)S(1)}, bf16[1024,128]{1,0:T(8,128)(2,1)S(1)}, u32[]{:S(2)}, u32[]{:S(2)}) collective-permute-start(bf16[1024,128]{1,0:T(8,128)(2,1)S(1)} %collective-permute-done.1.refs_2_), channel_id=1, source_target_pairs={{1,0},{2,1},{3,2},{4,3},{5,4},{6,5},{7,6},{8,7},{9,8},{10,9},{11,1... | collective-permute-start | bytes 786440 | tf_op jit(solution)/shard_map/ppermute | solution.py:143
  51.2 0.0 all-to-all-done
  51.2 0.2 constant_dynamic-slice_fusion
  51.4 0.0 collective-permute-done.refs_1_
  51.4 2.4 %shard_map.30.total_ref = f32[1024,2048]{1,0:T(8,128)S(1)} custom-call(bf16[1024,128]{1,0:T(8,128)(2,1)S(1)} %shard_map.28.refs_0_, bf16[1024,128]{1,0:T(8,128)(2,1)S(1)} %collective-permute-done.refs_1_, bf16[1024,128]{1,0:T(8,128)(2,1)S(1)} %collective-permute-done.1.refs_2_, bf16[128,2048]{1,0:T(8,128)(2,1)S(1)} %bitcast.17, ...), custom_call_target="tpu_custom_call" | custom-call | flops 1610612736 | bytes 8388608 | tf_op jit(solution)/shard_map/pallas_call | solution.py:88
  53.8 1.3 %collective-permute-done.2.across_ref = bf16[1024,128]{1,0:T(8,128)(2,1)S(1)} collective-permute-done((bf16[1024,128]{1,0:T(8,128)(2,1)S(1)}, bf16[1024,128]{1,0:T(8,128)(2,1)S(1)}, u32[]{:S(2)}, u32[]{:S(2)}) %collective-permute-start.2) | collective-permute-done | bytes 262176 | tf_op jit(solution)/shard_map/ppermute | solution.py:143
  55.0 2.4 %shard_map.31 = bf16[1024,2048]{1,0:T(8,128)(2,1)} custom-call(f32[1024,2048]{1,0:T(8,128)S(1)} %shard_map.30.total_ref, bf16[1024,128]{1,0:T(8,128)(2,1)S(1)} %collective-permute-done.2.across_ref, bf16[128,2048]{1,0:T(8,128)(2,1)S(1)} %bitcast.14), custom_call_target="tpu_custom_call" | custom-call | flops 1073741824 | bytes 12582912 | tf_op jit(solution)/shard_map/pallas_call | solution.py:125
Async XLA Ops:
  0.0 0.8 %copy-start = (bf16[16,2048]{1,0:T(8,128)(2,1)S(1)}, bf16[16,2048]{1,0:T(8,128)(2,1)}, u32[]{:S(2)}) copy-start(bf16[16,2048]{1,0:T(8,128)(2,1)} %block_ref.1) | copy-start | bytes 196612
  2.2 9.8 %copy-start.1 = (bf16[1024,32]{0,1:T(8,128)(2,1)S(1)}, bf16[1024,32]{0,1:T(8,128)(2,1)}, u32[]{:S(2)}) copy-start(bf16[1024,32]{0,1:T(8,128)(2,1)} %param.2) | copy-start | bytes 196612
  2.2 48.9 %all-to-all-start = ((bf16[32,16,2048]{2,1,0:T(8,128)(2,1)}), bf16[32,16,2048]{2,1,0:T(8,128)(2,1)S(1)}, u32[]{:S(2)}, u32[]{:S(2)}) async-start(bf16[32,16,2048]{2,1,0:T(8,128)(2,1)} %shard_map.29), calls=%async_computation | async-start | bytes 4194304 | tf_op jit(solution)/shard_map/all_to_all | solution.py:150
  37.6 8.3 %collective-permute-start.1 = (bf16[1024,128]{1,0:T(8,128)(2,1)S(1)}, bf16[1024,128]{1,0:T(8,128)(2,1)S(1)}, u32[]{:S(2)}, u32[]{:S(2)}) collective-permute-start(bf16[1024,128]{1,0:T(8,128)(2,1)S(1)} %shard_map.28.refs_0_), channel_id=1, source_target_pairs={{1,0},{2,1},{3,2},{4,3},{5,4},{6,5},{7,6},{8,7},{9,8},{10,9},{11,1... | collective-permute-start | bytes 786440 | tf_op jit(solution)/shard_map/ppermute | solution.py:143
  41.7 9.7 %collective-permute-start = (bf16[1024,128]{1,0:T(8,128)(2,1)S(1)}, bf16[1024,128]{1,0:T(8,128)(2,1)S(1)}, u32[]{:S(2)}, u32[]{:S(2)}) collective-permute-start(bf16[1024,128]{1,0:T(8,128)(2,1)S(1)} %shard_map.28.refs_0_), channel_id=1, source_target_pairs={{15,0},{0,1},{1,2},{2,3},{3,4},{4,5},{5,6},{6,7},{7,8},{8,9},{9,10... | collective-permute-start | bytes 786440 | tf_op jit(solution)/shard_map/ppermute | solution.py:143
  45.9 9.2 %collective-permute-start.2 = (bf16[1024,128]{1,0:T(8,128)(2,1)S(1)}, bf16[1024,128]{1,0:T(8,128)(2,1)S(1)}, u32[]{:S(2)}, u32[]{:S(2)}) collective-permute-start(bf16[1024,128]{1,0:T(8,128)(2,1)S(1)} %collective-permute-done.1.refs_2_), channel_id=1, source_target_pairs={{1,0},{2,1},{3,2},{4,3},{5,4},{6,5},{7,6},{8,7},{9,8},{10,9},{11,1... | collective-permute-start | bytes 786440 | tf_op jit(solution)/shard_map/ppermute | solution.py:143
